TPU v7x, 256 devices: a whole 4x4x8 slice. The times are simulated.
256 devices in a mesh: dom: 16 (over x, y_lo, core), space: 16 (over y_hi, z).
Axes of the slice: x: 4, y: 4 (y_hi: 2, y_lo: 2; y = y_hi * 2 + y_lo), z: 8, core: 2. Of those that a mesh axis runs over, the one named last changes fastest.
Arguments:
- ancestor: int32 [64], replicated, may hold values from 0 to 63, as said below
- state: float32 [64, 3, 256, 2048], P('dom', None, 'space'), may hold values from -6 to 6
- jitter: float32 [64, 3, 256, 2048], P('dom', None, 'space'), may hold values from -4 to 4
- depth: float32 [256, 2048], P('space'), may hold values from 0.5 to 2
- coriolis: float32 [256, 2048], P('space'), may hold values from -1 to 1
- drag: float32 [256, 2048], P('space'), may hold values from 0.1 to 1
Outputs:
- forecast: float32 [64, 3, 256, 2048], P('dom', None, 'space')
Inputs may be any that keep to these rules, and one draw needn't show every extreme that they name: In-place replacement: every particle either keeps its slot (ancestor[j] = j) or is replaced by a survivor p with ancestor[p] = p and p != j; a survivor is the ancestor of at most two new particles. Among the particles k*4 to k*4 + 3, at most 2 are ancestors of a particle other than themselves, and in every draw some such block has exactly 2.
All inputs are finite; a program needn't handle non-finite values.
Results may differ from a plain program's by a relative error of at most 0.00007.
Values sent between devices are 32-bit elements; how exact they have to be, the bound alone decides.
No kernel may reach another device: no remote copies, remote signals or barrier semaphores. Data moves between devices by JAX's collectives and lax.ppermute only.
A program may use at most 128 MiB of HBM per device.

v0:
```python
import jax
import jax.numpy as jnp
from jax import lax
from jax.sharding import PartitionSpec as P

STEPS = 4
time_step = 0.3


def extended(cells, sides, width):
    for axis, dim in sides:
        count = lax.axis_size(axis)
        head = lax.slice_in_dim(cells, 0, width, axis=dim)
        tail = lax.slice_in_dim(cells, cells.shape[dim] - width, cells.shape[dim], axis=dim)
        cells = jnp.concatenate(
            [
                lax.ppermute(tail, axis, [(i, (i + 1) % count) for i in range(count)]),
                cells,
                lax.ppermute(head, axis, [((i + 1) % count, i) for i in range(count)]),
            ],
            axis=dim,
        )
    return cells


def diff_zero(values):
    padded = jnp.pad(values, [(0, 0)] * (values.ndim - 1) + [(1, 1)])
    return 0.5 * (padded[..., 2:] - padded[..., :-2])


def diff_edge(values):
    padded = jnp.pad(values, [(0, 0)] * (values.ndim - 1) + [(1, 1)], mode="edge")
    return 0.5 * (padded[..., 2:] - padded[..., :-2])


def local(ancestor, state, jitter, depth, coriolis, drag):
    members = state.shape[0]
    myself = lax.axis_index("dom")
    wanted = lax.dynamic_slice_in_dim(ancestor, myself * members, members)
    piece = lax.all_gather(state, "dom", axis=0, tiled=True)
    take_count = piece.shape[0]
    select = (wanted[:, None] == jnp.arange(take_count, dtype=jnp.int32)[None, :]).astype(
        jnp.float32
    )
    copied = jnp.einsum("jk,kfrc->jfrc", select, piece, precision=lax.Precision.HIGHEST)
    fields = copied + jitter
    height, across, along = (fields[:, 0], fields[:, 1], fields[:, 2])
    for count in range(STEPS):
        flux = depth * along
        padded = extended(flux, (("space", 1),), 1)
        height_new = height - time_step * (
            diff_zero(depth * across) + 0.5 * (padded[:, 2:] - padded[:, :-2])
        )
        rimmed = extended(height_new, (("space", 1),), 1)
        across_new = (across + time_step * (coriolis * along - diff_edge(height_new))) / (
            1.0 + time_step * drag
        )
        along_new = (
            along + time_step * (-coriolis * across - 0.5 * (rimmed[:, 2:] - rimmed[:, :-2]))
        ) / (1.0 + time_step * drag)
        height, across, along = (height_new, across_new, along_new)
    return jnp.stack([height, across, along], axis=1)


def solution(mesh):
    placed = (
        P(),
        P("dom", None, "space", None),
        P("dom", None, "space", None),
        P("space", None),
        P("space", None),
        P("space", None),
    )
    return jax.shard_map(
        local, mesh=mesh, in_specs=placed, out_specs=P("dom", None, "space", None), check_vma=False
    )
```

profile of v0, /device:TPU:2, one launch (start us, length us, event | category | flops | bytes accessed | tf_op | source)
XLA Modules:
  0.0 258.6 jit_solution(7539135098943396371)
XLA Ops:
  7.4 138.2 %all-gather.2.cloned.1.call-done = f32[64,3,16,2048]{3,2,1,0:T(8,128)} async-done(((f32[4,3,16,2048]{3,2,1,0:T(8,128)}), f32[64,3,16,2048]{3,2,1,0:T(8,128)}) %all-gather.2.cloned.1.call-update) | async-done | bytes 25165840 | tf_op jit(solution)/shard_map/all_gather | solution.py:40
  145.6 29.7 %fusion.2 = f32[4,3,16,2048]{3,0,2,1:T(4,128)S(1)} fusion(f32[64,3,16,2048]{3,2,1,0:T(8,128)} %all-gather.2.cloned.1.call-done, f32[4,3,16,2048]{3,2,1,0:T(8,128)S(1)} %copy-done.2, s32[4]{0:T(128)S(1)} %dynamic_slice.3), kind=kOutput, calls=%fused_computation.2 | convolution fusion | flops 302383360 | bytes 28311568 | tf_op jit(solution)/shard_map/jk,kfrc->jfrc/dot_general | solution.py:45
  175.5 5.8 %collective-permute-start = (f32[4,1,2048]{2,0,1:T(4,128)S(1)}, f32[4,1,2048]{2,0,1:T(4,128)S(1)}, u32[]{:S(2)}, u32[]{:S(2)}) collective-permute-start(f32[4,1,2048]{2,0,1:T(4,128)S(1)} %get-tuple-element.49), channel_id=1, source_target_pairs={{1,0},{2,1},{3,2},{4,3},{5,4},{6,5},{7,6},{8,7},{9,8},{10,9},{11,1... | collective-permute-start | bytes 98312 | tf_op jit(solution)/shard_map/ppermute | solution.py:19
  183.0 5.9 %collective-permute-done.1 = f32[4,1,2048]{2,0,1:T(4,128)S(1)} collective-permute-done((f32[4,1,2048]{2,0,1:T(4,128)S(1)}, f32[4,1,2048]{2,0,1:T(4,128)S(1)}, u32[]{:S(2)}, u32[]{:S(2)}) %collective-permute-start.1) | collective-permute-done | bytes 32800 | tf_op jit(solution)/shard_map/ppermute | solution.py:17
  189.6 2.0 collective-permute-start.3
  191.7 1.8 collective-permute-done.2
  193.5 3.7 %collective-permute-done.3 = f32[4,1,2048]{2,0,1:T(4,128)S(1)} collective-permute-done((f32[4,1,2048]{2,0,1:T(4,128)S(1)}, f32[4,1,2048]{2,0,1:T(4,128)S(1)}, u32[]{:S(2)}, u32[]{:S(2)}) %collective-permute-start.3) | collective-permute-done | bytes 32800 | tf_op jit(solution)/shard_map/ppermute | solution.py:17
  198.3 2.0 collective-permute-start.5
  200.3 1.9 collective-permute-done.4
  202.2 3.7 %collective-permute-done.5 = f32[4,1,2048]{2,0,1:T(4,128)S(1)} collective-permute-done((f32[4,1,2048]{2,0,1:T(4,128)S(1)}, f32[4,1,2048]{2,0,1:T(4,128)S(1)}, u32[]{:S(2)}, u32[]{:S(2)}) %collective-permute-start.5) | collective-permute-done | bytes 32800 | tf_op jit(solution)/shard_map/ppermute | solution.py:17
  206.6 2.0 collective-permute-start.7
  208.7 1.8 collective-permute-done.6
  210.5 3.7 %collective-permute-done.7 = f32[4,1,2048]{2,0,1:T(4,128)S(1)} collective-permute-done((f32[4,1,2048]{2,0,1:T(4,128)S(1)}, f32[4,1,2048]{2,0,1:T(4,128)S(1)}, u32[]{:S(2)}, u32[]{:S(2)}) %collective-permute-start.7) | collective-permute-done | bytes 32800 | tf_op jit(solution)/shard_map/ppermute | solution.py:17
  215.3 2.0 collective-permute-start.9
  217.3 1.9 collective-permute-done.8
  219.2 3.7 %collective-permute-done.9 = f32[4,1,2048]{2,0,1:T(4,128)S(1)} collective-permute-done((f32[4,1,2048]{2,0,1:T(4,128)S(1)}, f32[4,1,2048]{2,0,1:T(4,128)S(1)}, u32[]{:S(2)}, u32[]{:S(2)}) %collective-permute-start.9) | collective-permute-done | bytes 32800 | tf_op jit(solution)/shard_map/ppermute | solution.py:17
  223.9 2.0 collective-permute-start.11
  227.8 3.7 %collective-permute-done.11 = f32[4,1,2048]{2,0,1:T(4,128)S(1)} collective-permute-done((f32[4,1,2048]{2,0,1:T(4,128)S(1)}, f32[4,1,2048]{2,0,1:T(4,128)S(1)}, u32[]{:S(2)}, u32[]{:S(2)}) %collective-permute-start.11) | collective-permute-done | bytes 32800 | tf_op jit(solution)/shard_map/ppermute | solution.py:17
  232.5 2.0 collective-permute-start.13
  234.5 1.9 collective-permute-done.12
  236.4 3.7 %collective-permute-done.13 = f32[4,1,2048]{2,0,1:T(4,128)S(1)} collective-permute-done((f32[4,1,2048]{2,0,1:T(4,128)S(1)}, f32[4,1,2048]{2,0,1:T(4,128)S(1)}, u32[]{:S(2)}, u32[]{:S(2)}) %collective-permute-start.13) | collective-permute-done | bytes 32800 | tf_op jit(solution)/shard_map/ppermute | solution.py:17
  240.9 2.0 collective-permute-start.15
  244.8 3.7 %collective-permute-done.15 = f32[4,1,2048]{2,0,1:T(4,128)S(1)} collective-permute-done((f32[4,1,2048]{2,0,1:T(4,128)S(1)}, f32[4,1,2048]{2,0,1:T(4,128)S(1)}, u32[]{:S(2)}, u32[]{:S(2)}) %collective-permute-start.15) | collective-permute-done | bytes 32800 | tf_op jit(solution)/shard_map/ppermute | solution.py:17
  249.7 2.1 copy.12
  (48 shorter events, 13.9 us)
Async XLA Ops:
  6.5 0.7 copy-start.4
  6.5 139.0 %copy-start.2 = (f32[4,3,16,2048]{3,2,1,0:T(8,128)S(1)}, f32[4,3,16,2048]{3,2,1,0:T(8,128)}, u32[]{:S(2)}) copy-start(f32[4,3,16,2048]{3,2,1,0:T(8,128)} %param.8) | copy-start | bytes 4718596
  6.5 139.0 %all-gather.2.cloned.1.call-start = ((), (), s32[]{:S(2)}) async-start(), calls=%async_computation | async-start | bytes 26738688 | tf_op jit(solution)/shard_map/all_gather | solution.py:40
  7.4 167.9 %copy-start.1 = (f32[16,2048]{1,0:T(8,128)S(1)}, f32[16,2048]{1,0:T(8,128)}, u32[]{:S(2)}) copy-start(f32[16,2048]{1,0:T(8,128)} %param.9) | copy-start | bytes 393220
  175.3 6.1 %copy-start.3 = (f32[16,2048]{1,0:T(8,128)S(1)}, f32[16,2048]{1,0:T(8,128)}, u32[]{:S(2)}) copy-start(f32[16,2048]{1,0:T(8,128)} %param.11) | copy-start | bytes 393220
  175.3 6.1 %copy-start = (f32[16,2048]{1,0:T(8,128)S(1)}, f32[16,2048]{1,0:T(8,128)}, u32[]{:S(2)}) copy-start(f32[16,2048]{1,0:T(8,128)} %param.10) | copy-start | bytes 393220
  175.5 7.4 %collective-permute-start = (f32[4,1,2048]{2,0,1:T(4,128)S(1)}, f32[4,1,2048]{2,0,1:T(4,128)S(1)}, u32[]{:S(2)}, u32[]{:S(2)}) collective-permute-start(f32[4,1,2048]{2,0,1:T(4,128)S(1)} %get-tuple-element.49), channel_id=1, source_target_pairs={{1,0},{2,1},{3,2},{4,3},{5,4},{6,5},{7,6},{8,7},{9,8},{10,9},{11,1... | collective-permute-start | bytes 98312 | tf_op jit(solution)/shard_map/ppermute | solution.py:19
  181.4 7.5 %collective-permute-start.1 = (f32[4,1,2048]{2,0,1:T(4,128)S(1)}, f32[4,1,2048]{2,0,1:T(4,128)S(1)}, u32[]{:S(2)}, u32[]{:S(2)}) collective-permute-start(f32[4,1,2048]{2,0,1:T(4,128)S(1)} %get-tuple-element.50), channel_id=1, source_target_pairs={{0,1},{1,2},{2,3},{3,4},{4,5},{5,6},{6,7},{7,8},{8,9},{9,10},{10,1... | collective-permute-start | bytes 98312 | tf_op jit(solution)/shard_map/ppermute | solution.py:17
  189.5 4.0 %collective-permute-start.2 = (f32[4,1,2048]{2,0,1:T(4,128)S(1)}, f32[4,1,2048]{2,0,1:T(4,128)S(1)}, u32[]{:S(2)}, u32[]{:S(2)}) collective-permute-start(f32[4,1,2048]{2,0,1:T(4,128)S(1)} %get-tuple-element.47), channel_id=1, source_target_pairs={{1,0},{2,1},{3,2},{4,3},{5,4},{6,5},{7,6},{8,7},{9,8},{10,9},{11,1... | collective-permute-start | bytes 98312 | tf_op jit(solution)/shard_map/ppermute | solution.py:19
  189.6 7.6 %collective-permute-start.3 = (f32[4,1,2048]{2,0,1:T(4,128)S(1)}, f32[4,1,2048]{2,0,1:T(4,128)S(1)}, u32[]{:S(2)}, u32[]{:S(2)}) collective-permute-start(f32[4,1,2048]{2,0,1:T(4,128)S(1)} %get-tuple-element.48), channel_id=1, source_target_pairs={{0,1},{1,2},{2,3},{3,4},{4,5},{5,6},{6,7},{7,8},{8,9},{9,10},{10,1... | collective-permute-start | bytes 98312 | tf_op jit(solution)/shard_map/ppermute | solution.py:17
  198.2 4.0 %collective-permute-start.4 = (f32[4,1,2048]{2,0,1:T(4,128)S(1)}, f32[4,1,2048]{2,0,1:T(4,128)S(1)}, u32[]{:S(2)}, u32[]{:S(2)}) collective-permute-start(f32[4,1,2048]{2,0,1:T(4,128)S(1)} %get-tuple-element.45), channel_id=1, source_target_pairs={{1,0},{2,1},{3,2},{4,3},{5,4},{6,5},{7,6},{8,7},{9,8},{10,9},{11,1... | collective-permute-start | bytes 98312 | tf_op jit(solution)/shard_map/ppermute | solution.py:19
  198.3 7.6 %collective-permute-start.5 = (f32[4,1,2048]{2,0,1:T(4,128)S(1)}, f32[4,1,2048]{2,0,1:T(4,128)S(1)}, u32[]{:S(2)}, u32[]{:S(2)}) collective-permute-start(f32[4,1,2048]{2,0,1:T(4,128)S(1)} %get-tuple-element.46), channel_id=1, source_target_pairs={{0,1},{1,2},{2,3},{3,4},{4,5},{5,6},{6,7},{7,8},{8,9},{9,10},{10,1... | collective-permute-start | bytes 98312 | tf_op jit(solution)/shard_map/ppermute | solution.py:17
  206.5 4.0 %collective-permute-start.6 = (f32[4,1,2048]{2,0,1:T(4,128)S(1)}, f32[4,1,2048]{2,0,1:T(4,128)S(1)}, u32[]{:S(2)}, u32[]{:S(2)}) collective-permute-start(f32[4,1,2048]{2,0,1:T(4,128)S(1)} %get-tuple-element.41), channel_id=1, source_target_pairs={{1,0},{2,1},{3,2},{4,3},{5,4},{6,5},{7,6},{8,7},{9,8},{10,9},{11,1... | collective-permute-start | bytes 98312 | tf_op jit(solution)/shard_map/ppermute | solution.py:19
  206.6 7.6 %collective-permute-start.7 = (f32[4,1,2048]{2,0,1:T(4,128)S(1)}, f32[4,1,2048]{2,0,1:T(4,128)S(1)}, u32[]{:S(2)}, u32[]{:S(2)}) collective-permute-start(f32[4,1,2048]{2,0,1:T(4,128)S(1)} %get-tuple-element.42), channel_id=1, source_target_pairs={{0,1},{1,2},{2,3},{3,4},{4,5},{5,6},{6,7},{7,8},{8,9},{9,10},{10,1... | collective-permute-start | bytes 98312 | tf_op jit(solution)/shard_map/ppermute | solution.py:17
  215.2 4.0 %collective-permute-start.8 = (f32[4,1,2048]{2,0,1:T(4,128)S(1)}, f32[4,1,2048]{2,0,1:T(4,128)S(1)}, u32[]{:S(2)}, u32[]{:S(2)}) collective-permute-start(f32[4,1,2048]{2,0,1:T(4,128)S(1)} %get-tuple-element.39), channel_id=1, source_target_pairs={{1,0},{2,1},{3,2},{4,3},{5,4},{6,5},{7,6},{8,7},{9,8},{10,9},{11,1... | collective-permute-start | bytes 98312 | tf_op jit(solution)/shard_map/ppermute | solution.py:19
  215.3 7.6 %collective-permute-start.9 = (f32[4,1,2048]{2,0,1:T(4,128)S(1)}, f32[4,1,2048]{2,0,1:T(4,128)S(1)}, u32[]{:S(2)}, u32[]{:S(2)}) collective-permute-start(f32[4,1,2048]{2,0,1:T(4,128)S(1)} %get-tuple-element.40), channel_id=1, source_target_pairs={{0,1},{1,2},{2,3},{3,4},{4,5},{5,6},{6,7},{7,8},{8,9},{9,10},{10,1... | collective-permute-start | bytes 98312 | tf_op jit(solution)/shard_map/ppermute | solution.py:17
  223.5 4.2 %collective-permute-start.10 = (f32[4,1,2048]{2,0,1:T(4,128)S(1)}, f32[4,1,2048]{2,0,1:T(4,128)S(1)}, u32[]{:S(2)}, u32[]{:S(2)}) collective-permute-start(f32[4,1,2048]{2,0,1:T(4,128)S(1)} %get-tuple-element.35), channel_id=1, source_target_pairs={{1,0},{2,1},{3,2},{4,3},{5,4},{6,5},{7,6},{8,7},{9,8},{10,9},{11,1... | collective-permute-start | bytes 98312 | tf_op jit(solution)/shard_map/ppermute | solution.py:19
  223.9 7.6 %collective-permute-start.11 = (f32[4,1,2048]{2,0,1:T(4,128)S(1)}, f32[4,1,2048]{2,0,1:T(4,128)S(1)}, u32[]{:S(2)}, u32[]{:S(2)}) collective-permute-start(f32[4,1,2048]{2,0,1:T(4,128)S(1)} %get-tuple-element.36), channel_id=1, source_target_pairs={{0,1},{1,2},{2,3},{3,4},{4,5},{5,6},{6,7},{7,8},{8,9},{9,10},{10,1... | collective-permute-start | bytes 98312 | tf_op jit(solution)/shard_map/ppermute | solution.py:17
  232.4 4.0 %collective-permute-start.12 = (f32[4,1,2048]{2,0,1:T(4,128)S(1)}, f32[4,1,2048]{2,0,1:T(4,128)S(1)}, u32[]{:S(2)}, u32[]{:S(2)}) collective-permute-start(f32[4,1,2048]{2,0,1:T(4,128)S(1)} %get-tuple-element.33), channel_id=1, source_target_pairs={{1,0},{2,1},{3,2},{4,3},{5,4},{6,5},{7,6},{8,7},{9,8},{10,9},{11,1... | collective-permute-start | bytes 98312 | tf_op jit(solution)/shard_map/ppermute | solution.py:19
  232.5 7.6 %collective-permute-start.13 = (f32[4,1,2048]{2,0,1:T(4,128)S(1)}, f32[4,1,2048]{2,0,1:T(4,128)S(1)}, u32[]{:S(2)}, u32[]{:S(2)}) collective-permute-start(f32[4,1,2048]{2,0,1:T(4,128)S(1)} %get-tuple-element.34), channel_id=1, source_target_pairs={{0,1},{1,2},{2,3},{3,4},{4,5},{5,6},{6,7},{7,8},{8,9},{9,10},{10,1... | collective-permute-start | bytes 98312 | tf_op jit(solution)/shard_map/ppermute | solution.py:17
  240.8 4.0 %collective-permute-start.14 = (f32[4,1,2048]{2,0,1:T(4,128)S(1)}, f32[4,1,2048]{2,0,1:T(4,128)S(1)}, u32[]{:S(2)}, u32[]{:S(2)}) collective-permute-start(f32[4,1,2048]{2,0,1:T(4,128)S(1)} %get-tuple-element.29), channel_id=1, source_target_pairs={{1,0},{2,1},{3,2},{4,3},{5,4},{6,5},{7,6},{8,7},{9,8},{10,9},{11,1... | collective-permute-start | bytes 98312 | tf_op jit(solution)/shard_map/ppermute | solution.py:19
  240.9 7.6 %collective-permute-start.15 = (f32[4,1,2048]{2,0,1:T(4,128)S(1)}, f32[4,1,2048]{2,0,1:T(4,128)S(1)}, u32[]{:S(2)}, u32[]{:S(2)}) collective-permute-start(f32[4,1,2048]{2,0,1:T(4,128)S(1)} %get-tuple-element.30), channel_id=1, source_target_pairs={{0,1},{1,2},{2,3},{3,4},{4,5},{5,6},{6,7},{7,8},{8,9},{9,10},{10,1... | collective-permute-start | bytes 98312 | tf_op jit(solution)/shard_map/ppermute | solution.py:17
Sparse Core Ops, SparseCore 0:
  9.2 136.3 all-gather.1
where the time goes:
time: 259 us
  waiting for transfers between devices  185 us (71%)
  matrix products  29.7 us (11%)
  starting transfers between devices  20.7 us (8%)
  between operations  13.6 us (5%)
  other arithmetic  6.78 us (3%)
    all_gather x1, waiting for transfers between devices, local(): piece = lax.all_gather(state, 'dom', axis=0, tiled=True)  138 us
    ppermute x8, waiting for transfers between devices, extended(): lax.ppermute(tail, axis, [(i, (i + 1) % count) for i in range(count)])  31.9 us
    dot_general x1, matrix products, local(): jnp.einsum('jk,kfrc->jfrc', select, piece, precision=lax.Precision.HIGHEST)  29.7 us
    ppermute x8, waiting for transfers between devices, extended(): lax.ppermute(head, axis, [((i + 1) % count, i) for i in range(count)])  14.4 us
    ppermute x8, starting transfers between devices, extended(): lax.ppermute(tail, axis, [(i, (i + 1) % count) for i in range(count)])  14.1 us
    ppermute x8, starting transfers between devices, extended(): lax.ppermute(head, axis, [((i + 1) % count, i) for i in range(count)])  6.64 us
  transfers between devices with their start and end apart: 17, of which 17 were waited for; matrix products, arithmetic and copies ran while one was open for 0% of the time, Pallas kernels for 0%

commit v1 on v0

--- a/solution.py
+++ b/solution.py
@@ -5,6 +5,13 @@
 
 STEPS = 4
 time_step = 0.3
+
+
+def swapped_in(shard, name, d):
+    size = lax.axis_size(name)
+    blocks = jnp.stack([shard for _ in range(size)])
+    blocks = lax.all_to_all(blocks, name, split_axis=0, concat_axis=0)
+    return jnp.concatenate(blocks, axis=d)
 
 
 def extended(cells, sides, width):
@@ -37,7 +44,7 @@
     members = state.shape[0]
     myself = lax.axis_index("dom")
     wanted = lax.dynamic_slice_in_dim(ancestor, myself * members, members)
-    piece = lax.all_gather(state, "dom", axis=0, tiled=True)
+    piece = swapped_in(state, "dom", 0)
     take_count = piece.shape[0]
     select = (wanted[:, None] == jnp.arange(take_count, dtype=jnp.int32)[None, :]).astype(
         jnp.float32

time: 259 us -> 573 us (2.21)
  the two profiles are of different devices: /device:TPU:2 before, /device:TPU:12 now
where the time goes in v1:
time: 573 us; the launch traced here: 572 us
  waiting for transfers between devices  459 us (80%)
  local copies, waits for them, and re-layouts  64 us (11%)
  starting transfers between devices  28.7 us (5%)
  matrix products  13.3 us (2%)
  other arithmetic  6.78 us (1%)
    all_to_all x1, waiting for transfers between devices, swapped_in(): blocks = lax.all_to_all(blocks, name, split_axis=0, concat_axis=0)  412 us
    ppermute x8, waiting for transfers between devices, extended(): lax.ppermute(tail, axis, [(i, (i + 1) % count) for i in range(count)])  32.1 us
    reshape x1, local copies, waits for them, and re-layouts, swapped_in(): return jnp.concatenate(blocks, axis=d)  29 us
    all_to_all x1, local copies, waits for them, and re-layouts, swapped_in(): blocks = lax.all_to_all(blocks, name, split_axis=0, concat_axis=0)  21 us
    ppermute x8, waiting for transfers between devices, extended(): lax.ppermute(head, axis, [((i + 1) % count, i) for i in range(count)])  14.4 us
    ppermute x8, starting transfers between devices, extended(): lax.ppermute(tail, axis, [(i, (i + 1) % count) for i in range(count)])  14.1 us
    dot_general x1, matrix products, local(): jnp.einsum('jk,kfrc->jfrc', select, piece, precision=lax.Precision.HIGHEST)  13.3 us
  transfers between devices with their start and end apart: 17, of which 17 were waited for; matrix products, arithmetic and copies ran while one was open for 0% of the time, Pallas kernels for 0%

profile of v1, /device:TPU:12, one launch (start us, length us, event | category | flops | bytes accessed | tf_op | source)
XLA Modules:
  0.0 572.0 jit_solution(3457916224089330800)
XLA Ops:
  0.0 2.4 copy.10
  2.4 9.0 %stack.10 = f32[16,4,3,16,2048]{4,1,3,2,0:T(4,128)} broadcast(f32[4,3,16,2048]{3,0,2,1:T(4,128)S(1)} %copy.10), dimensions={1,2,3,4} | broadcast | bytes 26738688 | tf_op jit(solution)/shard_map/stack | solution.py:12
  11.5 7.6 %all-to-all-start = ((f32[16,4,3,16,2048]{4,1,3,2,0:T(4,128)}), f32[16,4,3,16,2048]{4,1,3,2,0:T(4,128)}, u32[]{:S(2)}, u32[]{:S(2)}) async-start(f32[16,4,3,16,2048]{4,1,3,2,0:T(4,128)} %stack.10), calls=%async_computation | async-start | bytes 50331648 | tf_op jit(solution)/shard_map/all_to_all | solution.py:13
  19.2 412.5 %all-to-all-done = f32[16,4,3,16,2048]{4,1,3,2,0:T(4,128)} async-done(((f32[16,4,3,16,2048]{4,1,3,2,0:T(4,128)}), f32[16,4,3,16,2048]{4,1,3,2,0:T(4,128)}, u32[]{:S(2)}, u32[]{:S(2)}) %all-to-all-start) | async-done | bytes 25165856 | tf_op jit(solution)/shard_map/all_to_all | solution.py:13
  431.6 21.0 %copy.11 = f32[16,4,3,16,2048]{4,1,0,3,2:T(4,128)} copy(f32[16,4,3,16,2048]{4,1,3,2,0:T(4,128)} %all-to-all-done) | data formatting | bytes 50331648 | tf_op jit(solution)/shard_map/all_to_all | solution.py:13
  452.7 29.0 %reshape.10 = f32[64,3,16,2048]{3,0,2,1:T(8,128)} reshape(f32[16,4,3,16,2048]{4,1,0,3,2:T(4,128)} %copy.11) | data formatting | bytes 50331648 | tf_op jit(solution)/shard_map/reshape | solution.py:14
  481.6 13.3 %convolution_add_fusion = f32[4,3,16,2048]{3,0,2,1:T(4,128)S(1)} fusion(f32[64,3,16,2048]{3,0,2,1:T(8,128)} %reshape.10, f32[4,3,16,2048]{3,2,1,0:T(8,128)S(1)} %copy-done.2, s32[4]{0:T(128)S(1)} %dynamic_slice.3), kind=kOutput, calls=%fused_computation | convolution fusion | flops 302383360 | bytes 28311568 | tf_op jit(solution)/shard_map/jk,kfrc->jfrc/dot_general | solution.py:52
  495.3 6.2 %collective-permute-start = (f32[4,1,2048]{2,0,1:T(4,128)S(1)}, f32[4,1,2048]{2,0,1:T(4,128)S(1)}, u32[]{:S(2)}, u32[]{:S(2)}) collective-permute-start(f32[4,1,2048]{2,0,1:T(4,128)S(1)} %get-tuple-element.49), channel_id=1, source_target_pairs={{1,0},{2,1},{3,2},{4,3},{5,4},{6,5},{7,6},{8,7},{9,8},{10,9},{11,1... | collective-permute-start | bytes 98312 | tf_op jit(solution)/shard_map/ppermute | solution.py:26
  503.1 5.9 %collective-permute-done.1 = f32[4,1,2048]{2,0,1:T(4,128)S(1)} collective-permute-done((f32[4,1,2048]{2,0,1:T(4,128)S(1)}, f32[4,1,2048]{2,0,1:T(4,128)S(1)}, u32[]{:S(2)}, u32[]{:S(2)}) %collective-permute-start.1) | collective-permute-done | bytes 32800 | tf_op jit(solution)/shard_map/ppermute | solution.py:24
  509.7 2.0 collective-permute-start.3
  513.6 3.7 collective-permute-done.3
  518.6 2.0 collective-permute-start.5
  522.5 3.7 collective-permute-done.5
  526.9 2.0 collective-permute-start.7
  530.8 3.7 collective-permute-done.7
  535.6 2.0 collective-permute-start.9
  539.5 3.7 collective-permute-done.9
  543.9 2.0 collective-permute-start.11
  547.8 3.7 collective-permute-done.11
  552.6 2.0 collective-permute-start.13
  556.5 3.7 collective-permute-done.13
  560.9 2.0 collective-permute-start.15
  564.8 3.9 collective-permute-done.15
  570.0 2.1 copy.13
  (51 shorter events, 22.5 us)
Async XLA Ops:
  11.5 7.6 %copy-start.4 = (s32[64]{0:T(128)S(1)}, s32[64]{0:T(128)}, u32[]{:S(2)}) copy-start(s32[64]{0:T(128)} %param.6) | copy-start | bytes 772
  11.5 420.2 %all-to-all-start = ((f32[16,4,3,16,2048]{4,1,3,2,0:T(4,128)}), f32[16,4,3,16,2048]{4,1,3,2,0:T(4,128)}, u32[]{:S(2)}, u32[]{:S(2)}) async-start(f32[16,4,3,16,2048]{4,1,3,2,0:T(4,128)} %stack.10), calls=%async_computation | async-start | bytes 50331648 | tf_op jit(solution)/shard_map/all_to_all | solution.py:13
  452.7 29.0 %copy-start.2 = (f32[4,3,16,2048]{3,2,1,0:T(8,128)S(1)}, f32[4,3,16,2048]{3,2,1,0:T(8,128)}, u32[]{:S(2)}) copy-start(f32[4,3,16,2048]{3,2,1,0:T(8,128)} %param.8) | copy-start | bytes 4718596
  481.6 13.3 %copy-start.1 = (f32[16,2048]{1,0:T(8,128)S(1)}, f32[16,2048]{1,0:T(8,128)}, u32[]{:S(2)}) copy-start(f32[16,2048]{1,0:T(8,128)} %param.9) | copy-start | bytes 393220
  495.0 6.5 %copy-start.3 = (f32[16,2048]{1,0:T(8,128)S(1)}, f32[16,2048]{1,0:T(8,128)}, u32[]{:S(2)}) copy-start(f32[16,2048]{1,0:T(8,128)} %param.11) | copy-start | bytes 393220
  495.0 6.5 %copy-start = (f32[16,2048]{1,0:T(8,128)S(1)}, f32[16,2048]{1,0:T(8,128)}, u32[]{:S(2)}) copy-start(f32[16,2048]{1,0:T(8,128)} %param.10) | copy-start | bytes 393220
  495.3 7.8 %collective-permute-start = (f32[4,1,2048]{2,0,1:T(4,128)S(1)}, f32[4,1,2048]{2,0,1:T(4,128)S(1)}, u32[]{:S(2)}, u32[]{:S(2)}) collective-permute-start(f32[4,1,2048]{2,0,1:T(4,128)S(1)} %get-tuple-element.49), channel_id=1, source_target_pairs={{1,0},{2,1},{3,2},{4,3},{5,4},{6,5},{7,6},{8,7},{9,8},{10,9},{11,1... | collective-permute-start | bytes 98312 | tf_op jit(solution)/shard_map/ppermute | solution.py:26
  501.5 7.5 %collective-permute-start.1 = (f32[4,1,2048]{2,0,1:T(4,128)S(1)}, f32[4,1,2048]{2,0,1:T(4,128)S(1)}, u32[]{:S(2)}, u32[]{:S(2)}) collective-permute-start(f32[4,1,2048]{2,0,1:T(4,128)S(1)} %get-tuple-element.50), channel_id=1, source_target_pairs={{0,1},{1,2},{2,3},{3,4},{4,5},{5,6},{6,7},{7,8},{8,9},{9,10},{10,1... | collective-permute-start | bytes 98312 | tf_op jit(solution)/shard_map/ppermute | solution.py:24
  509.7 4.0 collective-permute-start.2
  509.7 7.6 %collective-permute-start.3 = (f32[4,1,2048]{2,0,1:T(4,128)S(1)}, f32[4,1,2048]{2,0,1:T(4,128)S(1)}, u32[]{:S(2)}, u32[]{:S(2)}) collective-permute-start(f32[4,1,2048]{2,0,1:T(4,128)S(1)} %get-tuple-element.48), channel_id=1, source_target_pairs={{0,1},{1,2},{2,3},{3,4},{4,5},{5,6},{6,7},{7,8},{8,9},{9,10},{10,1... | collective-permute-start | bytes 98312 | tf_op jit(solution)/shard_map/ppermute | solution.py:24
  518.3 4.2 collective-permute-start.4
  518.6 7.6 %collective-permute-start.5 = (f32[4,1,2048]{2,0,1:T(4,128)S(1)}, f32[4,1,2048]{2,0,1:T(4,128)S(1)}, u32[]{:S(2)}, u32[]{:S(2)}) collective-permute-start(f32[4,1,2048]{2,0,1:T(4,128)S(1)} %get-tuple-element.46), channel_id=1, source_target_pairs={{0,1},{1,2},{2,3},{3,4},{4,5},{5,6},{6,7},{7,8},{8,9},{9,10},{10,1... | collective-permute-start | bytes 98312 | tf_op jit(solution)/shard_map/ppermute | solution.py:24
  526.8 4.0 collective-permute-start.6
  526.9 7.6 %collective-permute-start.7 = (f32[4,1,2048]{2,0,1:T(4,128)S(1)}, f32[4,1,2048]{2,0,1:T(4,128)S(1)}, u32[]{:S(2)}, u32[]{:S(2)}) collective-permute-start(f32[4,1,2048]{2,0,1:T(4,128)S(1)} %get-tuple-element.42), channel_id=1, source_target_pairs={{0,1},{1,2},{2,3},{3,4},{4,5},{5,6},{6,7},{7,8},{8,9},{9,10},{10,1... | collective-permute-start | bytes 98312 | tf_op jit(solution)/shard_map/ppermute | solution.py:24
  535.5 4.0 collective-permute-start.8
  535.6 7.6 %collective-permute-start.9 = (f32[4,1,2048]{2,0,1:T(4,128)S(1)}, f32[4,1,2048]{2,0,1:T(4,128)S(1)}, u32[]{:S(2)}, u32[]{:S(2)}) collective-permute-start(f32[4,1,2048]{2,0,1:T(4,128)S(1)} %get-tuple-element.40), channel_id=1, source_target_pairs={{0,1},{1,2},{2,3},{3,4},{4,5},{5,6},{6,7},{7,8},{8,9},{9,10},{10,1... | collective-permute-start | bytes 98312 | tf_op jit(solution)/shard_map/ppermute | solution.py:24
  543.8 4.0 collective-permute-start.10
  543.9 7.6 %collective-permute-start.11 = (f32[4,1,2048]{2,0,1:T(4,128)S(1)}, f32[4,1,2048]{2,0,1:T(4,128)S(1)}, u32[]{:S(2)}, u32[]{:S(2)}) collective-permute-start(f32[4,1,2048]{2,0,1:T(4,128)S(1)} %get-tuple-element.36), channel_id=1, source_target_pairs={{0,1},{1,2},{2,3},{3,4},{4,5},{5,6},{6,7},{7,8},{8,9},{9,10},{10,1... | collective-permute-start | bytes 98312 | tf_op jit(solution)/shard_map/ppermute | solution.py:24
  552.5 4.0 collective-permute-start.12
  552.6 7.6 %collective-permute-start.13 = (f32[4,1,2048]{2,0,1:T(4,128)S(1)}, f32[4,1,2048]{2,0,1:T(4,128)S(1)}, u32[]{:S(2)}, u32[]{:S(2)}) collective-permute-start(f32[4,1,2048]{2,0,1:T(4,128)S(1)} %get-tuple-element.34), channel_id=1, source_target_pairs={{0,1},{1,2},{2,3},{3,4},{4,5},{5,6},{6,7},{7,8},{8,9},{9,10},{10,1... | collective-permute-start | bytes 98312 | tf_op jit(solution)/shard_map/ppermute | solution.py:24
  560.8 4.0 collective-permute-start.14
  560.9 7.8 %collective-permute-start.15 = (f32[4,1,2048]{2,0,1:T(4,128)S(1)}, f32[4,1,2048]{2,0,1:T(4,128)S(1)}, u32[]{:S(2)}, u32[]{:S(2)}) collective-permute-start(f32[4,1,2048]{2,0,1:T(4,128)S(1)} %get-tuple-element.30), channel_id=1, source_target_pairs={{0,1},{1,2},{2,3},{3,4},{4,5},{5,6},{6,7},{7,8},{8,9},{9,10},{10,1... | collective-permute-start | bytes 98312 | tf_op jit(solution)/shard_map/ppermute | solution.py:24
